TPU v7x, 32 devices: a whole 2x2x4 slice. The times are simulated.
32 devices in a mesh: rx: 16 (over z, y, core), tm: 2 (over x).
Axes of the slice: x: 2, y: 2, z: 4, core: 2. Of those that a mesh axis runs over, the one named last changes fastest.
Arguments:
- signals: float32 [2, 16, 131072], P(None, 'rx', 'tm'), may hold values from -6 to 6
Outputs:
- ambiguity: float32 [256, 2, 16, 4, 1, 256], P('tm', None, 'rx')
All inputs are finite; a program needn't handle non-finite values.
Results may differ from a plain program's by a relative error of at most 0.0003.
Values sent between devices are 32-bit elements; how exact they have to be, the bound alone decides.
No kernel may reach another device: no remote copies, remote signals or barrier semaphores. Data moves between devices by JAX's collectives and lax.ppermute only.
A program may use at most 64 MiB of HBM per device.

v0:
```python
import functools
import math

import jax
import jax.numpy as jnp
import numpy as np
from jax import lax
from jax.experimental import pallas as pl
from jax.experimental.pallas import tpu as pltpu
from jax.sharding import PartitionSpec as P


SEG_LEN = 4096
LAGS = 256
DOPLEN = 512
DOPK = 256
OFFS = 4

HALF = LAGS // 2
BLOCK = LAGS
WINDOW = 2 * LAGS
BLOCKS = SEG_LEN // BLOCK
ROWS = SEG_LEN // HALF
STORES = 4

VMEM = pl.BlockSpec(memory_space=pltpu.VMEM)
SMEM = pl.BlockSpec(memory_space=pltpu.SMEM)
HBM = pl.BlockSpec(memory_space=pltpu.HBM)
ANY = pl.BlockSpec(memory_space=pl.ANY)


def limit(mib):
    return pltpu.CompilerParams(vmem_limit_bytes=mib << 20)


RELAYED = (0, 2, 3)


def halves(table):
    high = table.astype(jnp.bfloat16)
    return jnp.asarray(high), jnp.asarray((table - high.astype(np.float64)).astype(jnp.bfloat16))


def trig(rows, columns):
    angle = 2.0 * math.pi / WINDOW * (np.outer(rows, columns) % WINDOW)
    return np.concatenate([np.cos(angle), np.sin(angle)], axis=0)


def split(value):
    high = value.astype(jnp.bfloat16)
    low = (value - high.astype(jnp.float32)).astype(jnp.bfloat16)
    return high, low


def split_table(value):
    high = lax.reduce_precision(value, exponent_bits=8, mantissa_bits=7)
    return high.astype(jnp.bfloat16), (value - high).astype(jnp.bfloat16)


def product(left, table_high, table_low):
    high, low = split(left)
    count = left.shape[0]
    both = jnp.dot(
        jnp.concatenate([high, low], axis=0), table_high, preferred_element_type=jnp.float32
    )
    rest = jnp.dot(high, table_low, preferred_element_type=jnp.float32)
    return both[:count] + both[count:] + rest


def gather_rows(piece_ref, scratch, row, firsts, segs):
    for plane in range(2):
        for position, first in enumerate(firsts):
            column = pl.ds(plane * BLOCK + position * HALF, HALF)
            for block in range(BLOCKS):
                half = (2 * block + first) % ROWS
                scratch[pl.ds(row + block * segs, segs), column] = piece_ref[
                    plane, pl.ds(half, segs, stride=ROWS), :
                ]


def transform(scratch, table_high, table_low):
    straight = scratch[...]
    count = straight.shape[0]
    crossed = jnp.concatenate([straight[:, BLOCK:], -straight[:, :BLOCK]], axis=1)
    out = product(jnp.concatenate([straight, crossed], axis=0), table_high[...], table_low[...])
    return out[:count], out[count:]


def swap_halves(value):
    return pltpu.roll(value, value.shape[0] // 2, axis=0)


def pair_sum(x_ref, x_slot, y_ref, y_slot, column, tile):
    re, im = None, None
    for row in range(0, x_ref.shape[1], tile):
        rows = pl.ds(row, tile)
        x_re = x_ref[x_slot, rows, pl.ds(column, HALF)]
        x_im = x_ref[x_slot, rows, pl.ds(WINDOW + column, HALF)]
        y_re = y_ref[y_slot, rows, pl.ds(column, HALF)]
        y_im = y_ref[y_slot, rows, pl.ds(WINDOW + column, HALF)]
        more_re = x_re * y_re + x_im * y_im
        more_im = x_im * y_re - x_re * y_im
        re, im = (more_re, more_im) if re is None else (re + more_re, im + more_im)
    return re, im


def near_pairs(segs, me, x_ref, y_ref, spectrum):
    tile = 2 * segs
    first_half = lax.broadcasted_iota(jnp.int32, (tile, HALF), 0) < segs
    zero = jnp.zeros((tile, HALF), jnp.float32)
    for q in range(OFFS):
        for column in range(0, WINDOW, HALF):
            sums = [
                pair_sum(x_ref, q ^ me, y_ref, (q - 1 - o) ^ me, column, tile)
                if o < q
                else (zero, zero)
                for o in range(OFFS)
            ]
            for o in range(0, OFFS, 2):
                rows = pl.ds((q * OFFS + o) * segs, tile)
                for part, base in ((0, 0), (1, WINDOW)):
                    a, b = sums[o][part], sums[o + 1][part]
                    spectrum[rows, pl.ds(base + column, HALF)] = jnp.where(
                        first_half, a, b
                    ) + swap_halves(jnp.where(first_half, b, a))


def far_pair(segs, q, r, x_ref, x_slot, y_ref, spectrum, first_row):
    tile = 2 * segs
    o = q + (OFFS - 1) - r

    @pl.when(q <= r)
    def _():
        second = lax.broadcasted_iota(jnp.int32, (tile, HALF), 0) >= segs
        mine = second == (lax.rem(o, 2) == 1)
        rows = pl.ds(pl.multiple_of(first_row + (o - lax.rem(o, 2)) * segs, tile), tile)
        for column in range(0, WINDOW, HALF):
            sums = pair_sum(x_ref, x_slot, y_ref, 0, column, tile)
            for value, base in zip(sums, (0, WINDOW)):
                columns = pl.ds(base + column, HALF)
                total = value + swap_halves(value)
                spectrum[rows, columns] = spectrum[rows, columns] + jnp.where(mine, total, 0.0)


def own_transform(piece, slot, table_high, table_low, x_out, y_out, scratch, segs):
    rows = BLOCKS * segs
    odd = lax.broadcasted_iota(jnp.int32, (rows, WINDOW), 1) % 2 == 1
    gather_rows(piece, scratch, 0, (1, 2), segs)
    gather_rows(piece, scratch, rows, (3, 0), segs)
    re, im = transform(scratch, table_high, table_low)
    y_out[slot, :, :WINDOW] = re[:rows]
    y_out[slot, :, WINDOW:] = im[:rows]
    x_out[slot, :, :WINDOW] = re[:rows] + jnp.where(odd, -re[rows:], re[rows:])
    x_out[slot, :, WINDOW:] = im[:rows] + jnp.where(odd, -im[rows:], im[rows:])


def own_kernel(segs, *refs):
    pieces, (table_high, table_low, x_out, y_out, scratch) = refs[:-5], refs[-5:]
    for slot, piece in enumerate(pieces):
        own_transform(piece, slot, table_high, table_low, x_out, y_out, scratch, segs)


def far_transform(piece, table_high, table_low, y_out, scratch, segs):
    gather_rows(piece, scratch, 0, (1, 2), segs)
    y_re, y_im = transform(scratch, table_high, table_low)
    y_out[0, :, :WINDOW] = y_re
    y_out[0, :, WINDOW:] = y_im


def far_kernel(segs, piece, table_high, table_low, y_out, scratch):
    far_transform(piece, table_high, table_low, y_out, scratch, segs)


def level_kernel(segs, place, piece, table_high, table_low, x_in, y_in, *refs):
    del x_in, y_in
    ready, (x_out, y_out, spectrum, scratch) = refs[:-4], refs[-4:]
    me = place[0]
    own_transform(piece, OFFS - 1, table_high, table_low, x_out, y_out, scratch, segs)
    near_pairs(segs, me, x_out, y_out, spectrum)
    for slot, y_ref in enumerate(ready):
        for x_slot in range(OFFS):
            q = me ^ x_slot
            far_pair(segs, q, me ^ slot, x_out, x_slot, y_ref, spectrum, q * (OFFS * segs))


def ahead_kernel(
    segs, slot, place, piece, table_high, table_low, x_ref, _, spectrum, y_scratch, scratch
):
    far_transform(piece, table_high, table_low, y_scratch, scratch, segs)
    me = place[0]
    for x_slot in range(OFFS):
        q = me ^ x_slot
        far_pair(segs, q, me ^ slot, x_ref, x_slot, y_scratch, spectrum, q * (OFFS * segs))


def finish(segs, parts, dy, place, x_ref, y_ref, sums, t_high, t_low, outs, spectrum, held):
    me, my_part = place[0], place[1]
    tile = 2 * segs
    lag_dev = LAGS // parts
    count = OFFS * segs
    slots = (2 * dy, 2 * dy + 1)
    for index, x_slot in enumerate(slots):
        q = me ^ x_slot
        spectrum[pl.ds(index * count, count), :] = sums[
            pl.ds(pl.multiple_of(q * count, count), count), :
        ]
        far_pair(segs, q, me ^ (OFFS - 1), x_ref, x_slot, y_ref, spectrum, index * count)
    s_re, s_im = spectrum[:, :WINDOW], spectrum[:, WINDOW:]
    left = jnp.concatenate(
        [jnp.concatenate([s_re, -s_im], axis=1), jnp.concatenate([s_im, s_re], axis=1)], axis=0
    )
    corr = product(left, t_high[...], t_low[...])
    wide_half = lax.broadcasted_iota(jnp.int32, (tile, LAGS), 0) < segs
    for index in range(len(slots)):
        for o in range(0, OFFS, 2):
            row = (index * OFFS + o) * segs
            re = corr[row : row + tile]
            im = corr[len(slots) * count + row : len(slots) * count + row + tile]
            first = jnp.where(wide_half, re, swap_halves(im))
            second = jnp.where(wide_half, swap_halves(re), im)
            for t in range(parts):
                lanes = slice(t * lag_dev, (t + 1) * lag_dev)
                held[index * parts + t, pl.ds(o * tile, tile), :] = first[:, lanes]
                held[index * parts + t, pl.ds((o + 1) * tile, tile), :] = second[:, lanes]
    send, keeps = outs[0], outs[1:]
    for dt, keep in enumerate(keeps):
        there = lax.rem(my_part + dt, parts)
        keep[...] = held[there]
        send[dt] = held[parts + there]


def first_kernel(segs, parts, place, piece, table_high, table_low, x_ref, sums, t_high, t_low, *refs):
    (y_out, *outs), (scratch, spectrum, held) = refs[:-3], refs[-3:]
    far_transform(piece, table_high, table_low, y_out, scratch, segs)
    finish(segs, parts, 1, place, x_ref, y_out, sums, t_high, t_low, outs, spectrum, held)


def second_kernel(segs, parts, place, y_ref, x_ref, sums, t_high, t_low, *refs):
    outs, (spectrum, held) = refs[:-2], refs[-2:]
    finish(segs, parts, 0, place, x_ref, y_ref, sums, t_high, t_low, outs, spectrum, held)


def doppler_kernel(segs, keep_ref, recv_ref, *refs):
    others, (table_high, table_low, out_ref, scratch, sems) = refs[:-5], refs[-5:]
    tile = 2 * segs
    lag_dev = keep_ref.shape[1]
    stride = scratch.shape[0] // lag_dev
    per = DOPK // HALF
    table = jnp.concatenate([table_high[...], table_high[...], table_low[...]], axis=0)
    outs = []
    for o in range(OFFS):
        rows = pl.ds(o * tile, tile)
        tiles = [keep_ref[rows, :], recv_ref[0, rows, :]]
        for other in others:
            tiles += [other[0, rows, :], other[1, rows, :]]
        high, low = split(jnp.concatenate(tiles, axis=0))
        left = jnp.concatenate([high, low, high], axis=0)
        outs.append(
            lax.dot_general(
                left, table, (((0,), (0,)), ((), ())), preferred_element_type=jnp.float32
            )
        )
    lags = lag_dev // STORES
    copies = []
    for store in range(STORES):
        base = store * lags
        for o in range(OFFS):
            for c in range(2):
                for f in range(per):
                    where = base * stride + (c * OFFS + o) * per + f
                    first = c * DOPK + f * HALF
                    scratch[pl.ds(where, lags, stride=stride), :] = outs[o][
                        base : base + lags, first : first + HALF
                    ]
        span = pl.ds(base * stride, lags * stride)
        copies.append(pltpu.make_async_copy(scratch.at[span], out_ref.at[span], sems.at[store]))
        copies[-1].start()
    for copy in copies:
        copy.wait()


def doppler_table(sources, seg_dev, segs, scale):
    segment = jnp.concatenate(
        [part * seg_dev + slot * segs + jnp.arange(segs, dtype=jnp.int32) for slot, part in sources]
    )
    frequency = jnp.arange(DOPK, dtype=jnp.int32) - DOPK // 2
    angle = (
        2.0 * math.pi / DOPLEN
        * (segment[:, None] * frequency[None, :] % DOPLEN).astype(jnp.float32)
    )
    cos, sin = (jnp.cos(angle) * scale, jnp.sin(angle) * scale)
    cos = cos.reshape(len(sources), 1, segs, DOPK)
    sin = sin.reshape(len(sources), 1, segs, DOPK)
    table = jnp.concatenate(
        [jnp.concatenate([cos, -sin], axis=3), jnp.concatenate([sin, cos], axis=3)], axis=1
    ).reshape(2 * len(sources) * segs, 2 * DOPK)
    return split_table(table)


def per_device(count, parts, signals):
    rec_dev, length = signals.shape[1], signals.shape[2]
    seg_dev = length // SEG_LEN
    segs = seg_dev // OFFS
    assert rec_dev == 1 and count % OFFS == 0 and seg_dev % OFFS == 0
    me = lax.axis_index("rx") % OFFS
    my_part = lax.axis_index("tm")
    place = jnp.stack([me, my_part]).astype(jnp.int32)

    def move(value, flip, ahead=0, later=0):
        pairs = []
        for r in range(count):
            for t in range(parts):
                to = ((r ^ flip) + ahead) % count
                pairs.append((r * parts + t, to * parts + (t + later) % parts))
        return lax.ppermute(value, ("rx", "tm"), pairs)

    raw = signals.reshape(2, seg_dev * ROWS, HALF)

    cuts = [
        lax.dynamic_slice_in_dim(raw, (me ^ slot) * (segs * ROWS), segs * ROWS, axis=1)
        for slot in range(OFFS)
    ]
    own = [cuts[0]]
    own += [move(cuts[slot], slot) for slot in range(1, OFFS)]
    far = [
        move(own[slot], 0, ahead=OFFS)
        if slot in RELAYED
        else move(cuts[slot], slot, ahead=OFFS)
        for slot in range(OFFS)
    ]

    frequency = np.arange(WINDOW)
    high, low = halves(trig(np.arange(BLOCK), frequency))
    t_high, t_low = halves(trig(frequency, np.arange(LAGS) - HALF) / WINDOW)

    rows = BLOCKS * segs
    last = OFFS - 1
    spectra = jax.ShapeDtypeStruct((OFFS, rows, 2 * WINDOW), jnp.float32)
    spectrum = jax.ShapeDtypeStruct((1, rows, 2 * WINDOW), jnp.float32)
    sums = jax.ShapeDtypeStruct((OFFS * OFFS * segs, 2 * WINDOW), jnp.float32)
    own_rows = pltpu.VMEM((2 * rows, 2 * BLOCK), jnp.float32)
    far_rows = pltpu.VMEM((rows, 2 * BLOCK), jnp.float32)
    x_own, y_own = pl.pallas_call(
        functools.partial(own_kernel, segs),
        out_shape=(spectra, spectra),
        in_specs=[VMEM] * (last + 2),
        out_specs=(VMEM, VMEM),
        scratch_shapes=[own_rows],
        compiler_params=limit(6),
        name="own",
    )(*own[:last], high, low)
    ready = [
        pl.pallas_call(
            functools.partial(far_kernel, segs),
            out_shape=spectrum,
            in_specs=[VMEM] * 3,
            out_specs=VMEM,
            scratch_shapes=[far_rows],
            compiler_params=limit(4),
            name="far",
        )(piece, high, low)
        for piece in far[: last - 1]
    ]
    x_own, _, total = pl.pallas_call(
        functools.partial(level_kernel, segs),
        out_shape=(spectra, spectra, sums),
        in_specs=[SMEM] + [VMEM] * (5 + len(ready)),
        out_specs=(VMEM, VMEM, VMEM),
        scratch_shapes=[own_rows],
        input_output_aliases={4: 0, 5: 1},
        compiler_params=limit(6),
        name="level",
    )(place, own[last], high, low, x_own, y_own, *ready)
    total = pl.pallas_call(
        functools.partial(ahead_kernel, segs, last - 1),
        out_shape=sums,
        in_specs=[SMEM] + [VMEM] * 5,
        out_specs=VMEM,
        scratch_shapes=[pltpu.VMEM(spectrum.shape, jnp.float32), far_rows],
        input_output_aliases={5: 0},
        compiler_params=limit(4),
        name="ahead",
    )(place, far[last - 1], high, low, x_own, total)

    lag_dev = LAGS // parts
    piece_rows = OFFS * 2 * segs
    sources = []
    for dy in range(2):
        for dt in range(parts):
            slot, part = me ^ (2 * dy), (my_part - dt) % parts
            sources += [(slot, part), (slot ^ 1, part)]
    scale = 1.0 / math.sqrt(2.0 * SEG_LEN * seg_dev * parts)
    d_high, d_low, total = lax.optimization_barrier(
        (*doppler_table(sources, seg_dev, segs, scale), total)
    )
    keep = jax.ShapeDtypeStruct((piece_rows, lag_dev), jnp.float32)
    leaving = (jax.ShapeDtypeStruct((parts, piece_rows, lag_dev), jnp.float32),) + (keep,) * parts
    working = [
        pltpu.VMEM((2 * OFFS * segs, 2 * WINDOW), jnp.float32),
        pltpu.VMEM((2 * parts, piece_rows, lag_dev), jnp.float32),
    ]
    y_last, *crossing = pl.pallas_call(
        functools.partial(first_kernel, segs, parts),
        out_shape=(spectrum, *leaving),
        in_specs=[SMEM] + [VMEM] * 7,
        out_specs=(VMEM,) * (2 + parts),
        scratch_shapes=[far_rows] + working,
        compiler_params=limit(6),
        name="first",
    )(place, far[last], high, low, x_own, total, t_high, t_low)
    staying = pl.pallas_call(
        functools.partial(second_kernel, segs, parts),
        out_shape=leaving,
        in_specs=[SMEM] + [VMEM] * 5,
        out_specs=(VMEM,) * (1 + parts),
        scratch_shapes=working,
        compiler_params=limit(6),
        name="second",
    )(place, y_last, x_own, total, t_high, t_low)
    got = {1: move(crossing[0], 1), 0: move(staying[0], 1)}
    kept = {1: crossing[1:], 0: staying[1:]}
    keep, recv = kept[0][0], got[0]
    others = [
        move(jnp.stack([kept[dy][dt], got[dy][dt]]), 2 * dy, later=dt)
        for dy in range(2)
        for dt in range(parts)
        if dy or dt
    ]
    out_rows = lag_dev * 2 * OFFS * DOPK // HALF
    out = pl.pallas_call(
        functools.partial(doppler_kernel, segs),
        out_shape=jax.ShapeDtypeStruct((out_rows, HALF), jnp.float32),
        in_specs=[VMEM] * (len(others) + 4),
        out_specs=ANY,
        scratch_shapes=[
            pltpu.VMEM((out_rows, HALF), jnp.float32),
            pltpu.SemaphoreType.DMA((STORES,)),
        ],
        compiler_params=limit(6),
        name="doppler",
    )(keep, recv, *others, d_high, d_low)
    return out.reshape(lag_dev, 2, 1, OFFS, 1, DOPK)


def solution(mesh):
    count, parts = mesh.shape["rx"], mesh.shape["tm"]

    def body(signals):
        return per_device(count, parts, signals)

    return jax.shard_map(
        body,
        mesh=mesh,
        in_specs=(P(None, "rx", "tm"),),
        out_specs=P("tm", None, "rx", None, None, None),
        check_vma=False,
    )
```

profile of v0, /device:TPU:0, one launch (start us, length us, event | category | flops | bytes accessed | tf_op | source)
XLA Modules:
  0.0 31.8 jit_solution(2610221835771067236)
XLA Ops:
  0.0 1.2 %constant_dynamic-slice_fusion = (f32[2,128,128]{2,1,0:T(8,128)S(1)}, f32[2,128,128]{2,1,0:T(8,128)S(1)}, f32[2,128,128]{2,1,0:T(8,128)S(1)}, f32[2,128,128]{2,1,0:T(8,128)S(1)}) fusion(f32[2,512,128]{2,1,0:T(8,128)} %bitcast.10, s32[]{:T(128)S(6)} %select_n.57, s32[]{:T(128)S(6)} %select_n.56, s32[]{:T(128)S(6)} %select_n.55, s32[]{:T(128)S(6)} %select_n.54), kind=kLoop, calls=%fused_computation.19 | loop fusion | bytes 1048592 | tf_op jit(solution)/shard_map/dynamic_slice | solution.py:320
  1.2 0.6 %collective-permute-start.2 = (f32[2,128,128]{2,1,0:T(8,128)S(1)}, f32[2,128,128]{2,1,0:T(8,128)S(1)}, u32[]{:S(2)}, u32[]{:S(2)}) collective-permute-start(f32[2,128,128]{2,1,0:T(8,128)S(1)} %get-tuple-element.34), channel_id=1, source_target_pairs={{0,2},{1,3},{2,0},{3,1},{4,6},{5,7},{6,4},{7,5},{8,10},{9,11},{10,... | collective-permute-start | bytes 393224 | tf_op jit(solution)/shard_map/ppermute | solution.py:315
  1.8 2.7 %collective-permute-start.5 = (f32[2,128,128]{2,1,0:T(8,128)S(1)}, f32[2,128,128]{2,1,0:T(8,128)S(1)}, u32[]{:S(2)}, u32[]{:S(2)}) collective-permute-start(f32[2,128,128]{2,1,0:T(8,128)S(1)} %get-tuple-element.34), channel_id=1, source_target_pairs={{0,10},{1,11},{2,8},{3,9},{4,14},{5,15},{6,12},{7,13},{8,18},{9,19... | collective-permute-start | bytes 393224 | tf_op jit(solution)/shard_map/ppermute | solution.py:315
  4.4 1.5 %collective-permute-start.3 = (f32[2,128,128]{2,1,0:T(8,128)S(1)}, f32[2,128,128]{2,1,0:T(8,128)S(1)}, u32[]{:S(2)}, u32[]{:S(2)}) collective-permute-start(f32[2,128,128]{2,1,0:T(8,128)S(1)} %get-tuple-element.33), channel_id=1, source_target_pairs={{0,4},{1,5},{2,6},{3,7},{4,0},{5,1},{6,2},{7,3},{8,12},{9,13},{10,... | collective-permute-start | bytes 393224 | tf_op jit(solution)/shard_map/ppermute | solution.py:315
  6.0 1.6 %collective-permute-start.4 = (f32[2,128,128]{2,1,0:T(8,128)S(1)}, f32[2,128,128]{2,1,0:T(8,128)S(1)}, u32[]{:S(2)}, u32[]{:S(2)}) collective-permute-start(f32[2,128,128]{2,1,0:T(8,128)S(1)} %get-tuple-element.35.refs_0_), channel_id=1, source_target_pairs={{0,8},{1,9},{2,10},{3,11},{4,12},{5,13},{6,14},{7,15},{8,16},{9,17... | collective-permute-start | bytes 393224 | tf_op jit(solution)/shard_map/ppermute | solution.py:315
  8.2 1.7 %collective-permute-done.3.refs_2_ = f32[2,128,128]{2,1,0:T(8,128)S(1)} collective-permute-done((f32[2,128,128]{2,1,0:T(8,128)S(1)}, f32[2,128,128]{2,1,0:T(8,128)S(1)}, u32[]{:S(2)}, u32[]{:S(2)}) %collective-permute-start.3) | collective-permute-done | bytes 131104 | tf_op jit(solution)/shard_map/ppermute | solution.py:315
  9.9 1.6 %collective-permute-start.6 = (f32[2,128,128]{2,1,0:T(8,128)S(1)}, f32[2,128,128]{2,1,0:T(8,128)S(1)}, u32[]{:S(2)}, u32[]{:S(2)}) collective-permute-start(f32[2,128,128]{2,1,0:T(8,128)S(1)} %collective-permute-done.3.refs_2_), channel_id=1, source_target_pairs={{0,8},{1,9},{2,10},{3,11},{4,12},{5,13},{6,14},{7,15},{8,16},{9,17... | collective-permute-start | bytes 393224 | tf_op jit(solution)/shard_map/ppermute | solution.py:315
  11.5 1.5 %collective-permute-done.piece = f32[2,128,128]{2,1,0:T(8,128)S(1)} collective-permute-done((f32[2,128,128]{2,1,0:T(8,128)S(1)}, f32[2,128,128]{2,1,0:T(8,128)S(1)}, u32[]{:S(2)}, u32[]{:S(2)}) %collective-permute-start) | collective-permute-done | bytes 131104 | tf_op jit(solution)/shard_map/ppermute | solution.py:315
  13.0 1.6 %collective-permute-start.1 = (f32[2,128,128]{2,1,0:T(8,128)S(1)}, f32[2,128,128]{2,1,0:T(8,128)S(1)}, u32[]{:S(2)}, u32[]{:S(2)}) collective-permute-start(f32[2,128,128]{2,1,0:T(8,128)S(1)} %collective-permute-done.piece), channel_id=1, source_target_pairs={{0,8},{1,9},{2,10},{3,11},{4,12},{5,13},{6,14},{7,15},{8,16},{9,17... | collective-permute-start | bytes 393224 | tf_op jit(solution)/shard_map/ppermute | solution.py:315
  14.7 1.8 %own.1 = (f32[4,64,1024]{2,1,0:T(8,128)S(1)}, f32[4,64,1024]{2,1,0:T(8,128)S(1)}) custom-call(f32[2,128,128]{2,1,0:T(8,128)S(1)} %get-tuple-element.35.refs_0_, f32[2,128,128]{2,1,0:T(8,128)S(1)} %collective-permute-done.2.refs_1_, f32[2,128,128]{2,1,0:T(8,128)S(1)} %collective-permute-done.3.refs_2_, bf16[512,512]{1,0:T(8,128)(2,1)S(1)} %copy-done, ...), custom_call_target="tpu_custom_call" | custom-call | tf_op jit(solution)/shard_map/own/pallas_call | solution.py:343
  16.5 0.4 %far.2.refs_0_ = f32[1,64,1024]{2,1,0:T(8,128)S(1)} custom-call(f32[2,128,128]{2,1,0:T(8,128)S(1)} %collective-permute-done.4.piece, bf16[512,512]{1,0:T(8,128)(2,1)S(1)} %copy-done, bf16[512,512]{1,0:T(8,128)(2,1)S(1)} %copy-done.1), custom_call_target="tpu_custom_call" | custom-call | tf_op jit(solution)/shard_map/far/pallas_call | solution.py:353
  16.9 0.4 %far.3.refs_1_ = f32[1,64,1024]{2,1,0:T(8,128)S(1)} custom-call(f32[2,128,128]{2,1,0:T(8,128)S(1)} %collective-permute-done.5.piece, bf16[512,512]{1,0:T(8,128)(2,1)S(1)} %copy-done, bf16[512,512]{1,0:T(8,128)(2,1)S(1)} %copy-done.1), custom_call_target="tpu_custom_call" | custom-call | tf_op jit(solution)/shard_map/far/pallas_call | solution.py:353
  17.4 1.6 %level.1 = (f32[4,64,1024]{2,1,0:T(8,128)S(1)}, f32[4,64,1024]{2,1,0:T(8,128)S(1)}, f32[64,1024]{1,0:T(8,128)S(1)}) custom-call(s32[2]{0:T(128)S(1)} %pad_add_fusion.place, f32[2,128,128]{2,1,0:T(8,128)S(1)} %collective-permute-done.piece, bf16[512,512]{1,0:T(8,128)(2,1)S(1)} %copy-done, ...), custom_call_target="tpu_custom_call", output_to_operand_aliasing={{0}: (4, {}), {1}: (5, {})} | custom-call | tf_op jit(solution)/shard_map/level/pallas_call | solution.py:364
  19.0 1.1 %ahead.1.sums = f32[64,1024]{1,0:T(8,128)S(1)} custom-call(s32[2]{0:T(128)S(1)} %pad_add_fusion.place, f32[2,128,128]{2,1,0:T(8,128)S(1)} %collective-permute-done.6.piece, bf16[512,512]{1,0:T(8,128)(2,1)S(1)} %copy-done, bf16[512,512]{1,0:T(8,128)(2,1)S(1)} %copy-done.1, ...), custom_call_target="tpu_custom_call", output_to_operand_aliasing={{}: (5, {})} | custom-call | tf_op jit(solution)/shard_map/ahead/pallas_call | solution.py:374
  20.2 1.6 %first.1 = (f32[1,64,1024]{2,1,0:T(8,128)S(1)}, f32[2,32,128]{2,1,0:T(8,128)S(1)}, f32[32,128]{1,0:T(8,128)S(1)}, f32[32,128]{1,0:T(8,128)S(1)}) custom-call(s32[2]{0:T(128)S(1)} %pad_add_fusion.place, f32[2,128,128]{2,1,0:T(8,128)S(1)} %collective-permute-done.1.piece, bf16[512,512]{1,0:T(8,128)(2,1)S(1)} %copy-done, bf16[512,512]{1,0:T(8,128)(2,1)S(1)} %copy-done.1, ...), custom_call_target="tpu_custom_call" | custom-call | tf_op jit(solution)/shard_map/first/pallas_call | solution.py:402
  21.9 1.0 %second.1 = (f32[2,32,128]{2,1,0:T(8,128)S(1)}, f32[32,128]{1,0:T(8,128)S(1)}, f32[32,128]{1,0:T(8,128)S(1)}) custom-call(s32[2]{0:T(128)S(1)} %pad_add_fusion.place, f32[1,64,1024]{2,1,0:T(8,128)S(1)} %get-tuple-element.24.y_ref, f32[4,64,1024]{2,1,0:T(8,128)S(1)} %get-tuple-element.21.x_ref, f32[64,1024]{1,0:T(8,128)S(1)} %ahead.1.sums, ...), custom_call_target="tpu_custom_call" | custom-call | tf_op jit(solution)/shard_map/second/pallas_call | solution.py:411
  22.9 0.6 %collective-permute-start.7 = (f32[2,32,128]{2,1,0:T(8,128)S(1)}, f32[2,32,128]{2,1,0:T(8,128)S(1)}, u32[]{:S(2)}, u32[]{:S(2)}) collective-permute-start(f32[2,32,128]{2,1,0:T(8,128)S(1)} %get-tuple-element.26), channel_id=1, source_target_pairs={{0,2},{1,3},{2,0},{3,1},{4,6},{5,7},{6,4},{7,5},{8,10},{9,11},{10,... | collective-permute-start | bytes 98312 | tf_op jit(solution)/shard_map/ppermute | solution.py:315
  23.4 2.2 %collective-permute-start.11 = (f32[2,32,128]{2,1,0:T(8,128)S(1)}, f32[2,32,128]{2,1,0:T(8,128)S(1)}, u32[]{:S(2)}, u32[]{:S(2)}) collective-permute-start(f32[2,32,128]{2,1,0:T(8,128)S(1)} %pad_maximum_fusion.2), channel_id=1, source_target_pairs={{0,5},{1,4},{2,7},{3,6},{4,1},{5,0},{6,3},{7,2},{8,13},{9,12},{10,... | collective-permute-start | bytes 98312 | tf_op jit(solution)/shard_map/ppermute | solution.py:315
  25.7 0.8 %collective-permute-start.10 = (f32[2,32,128]{2,1,0:T(8,128)S(1)}, f32[2,32,128]{2,1,0:T(8,128)S(1)}, u32[]{:S(2)}, u32[]{:S(2)}) collective-permute-start(f32[2,32,128]{2,1,0:T(8,128)S(1)} %pad_maximum_fusion.1), channel_id=1, source_target_pairs={{0,4},{1,5},{2,6},{3,7},{4,0},{5,1},{6,2},{7,3},{8,12},{9,13},{10,... | collective-permute-start | bytes 98312 | tf_op jit(solution)/shard_map/ppermute | solution.py:315
  26.5 0.6 %collective-permute-start.8 = (f32[2,32,128]{2,1,0:T(8,128)S(1)}, f32[2,32,128]{2,1,0:T(8,128)S(1)}, u32[]{:S(2)}, u32[]{:S(2)}) collective-permute-start(f32[2,32,128]{2,1,0:T(8,128)S(1)} %pad_maximum_fusion), channel_id=1, source_target_pairs={{0,1},{1,0},{2,3},{3,2},{4,5},{5,4},{6,7},{7,6},{8,9},{9,8},{10,11... | collective-permute-start | bytes 98312 | tf_op jit(solution)/shard_map/ppermute | solution.py:315
  27.1 1.3 %collective-permute-done.11.refs_2_ = f32[2,32,128]{2,1,0:T(8,128)S(1)} collective-permute-done((f32[2,32,128]{2,1,0:T(8,128)S(1)}, f32[2,32,128]{2,1,0:T(8,128)S(1)}, u32[]{:S(2)}, u32[]{:S(2)}) %collective-permute-start.11) | collective-permute-done | bytes 32800 | tf_op jit(solution)/shard_map/ppermute | solution.py:315
  28.3 1.2 %collective-permute-done.10.refs_1_ = f32[2,32,128]{2,1,0:T(8,128)S(1)} collective-permute-done((f32[2,32,128]{2,1,0:T(8,128)S(1)}, f32[2,32,128]{2,1,0:T(8,128)S(1)}, u32[]{:S(2)}, u32[]{:S(2)}) %collective-permute-start.10) | collective-permute-done | bytes 32800 | tf_op jit(solution)/shard_map/ppermute | solution.py:315
  29.6 0.9 %collective-permute-done.8.refs_0_ = f32[2,32,128]{2,1,0:T(8,128)S(1)} collective-permute-done((f32[2,32,128]{2,1,0:T(8,128)S(1)}, f32[2,32,128]{2,1,0:T(8,128)S(1)}, u32[]{:S(2)}, u32[]{:S(2)}) %collective-permute-start.8) | collective-permute-done | bytes 32800 | tf_op jit(solution)/shard_map/ppermute | solution.py:315
  30.5 1.4 %doppler.1 = f32[2048,128]{1,0:T(8,128)} custom-call(f32[32,128]{1,0:T(8,128)S(1)} %get-tuple-element.25.keep_ref, f32[2,32,128]{2,1,0:T(8,128)S(1)} %collective-permute-done.7.recv_ref, f32[2,32,128]{2,1,0:T(8,128)S(1)} %collective-permute-done.8.refs_0_, f32[2,32,128]{2,1,0:T(8,128)S(1)} %collective-permute-done.10.refs_1_, ...), custom_call_target="tpu_custom_call" | custom-call | tf_op jit(solution)/shard_map/doppler/pallas_call | solution.py:430
  (34 shorter events, 0.8 us)
Async XLA Ops:
  0.0 14.7 %copy-start.1 = (bf16[512,512]{1,0:T(8,128)(2,1)S(1)}, bf16[512,512]{1,0:T(8,128)(2,1)}, u32[]{:S(2)}) copy-start(bf16[512,512]{1,0:T(8,128)(2,1)} %constant.78.clone.refs_4_.table_low) | copy-start | bytes 1572868
  1.2 13.5 %copy-start = (bf16[512,512]{1,0:T(8,128)(2,1)S(1)}, bf16[512,512]{1,0:T(8,128)(2,1)}, u32[]{:S(2)}) copy-start(bf16[512,512]{1,0:T(8,128)(2,1)} %constant.77.clone.refs_3_.table_high) | copy-start | bytes 1572868
  1.2 13.5 %collective-permute-start.2 = (f32[2,128,128]{2,1,0:T(8,128)S(1)}, f32[2,128,128]{2,1,0:T(8,128)S(1)}, u32[]{:S(2)}, u32[]{:S(2)}) collective-permute-start(f32[2,128,128]{2,1,0:T(8,128)S(1)} %get-tuple-element.34), channel_id=1, source_target_pairs={{0,2},{1,3},{2,0},{3,1},{4,6},{5,7},{6,4},{7,5},{8,10},{9,11},{10,... | collective-permute-start | bytes 393224 | tf_op jit(solution)/shard_map/ppermute | solution.py:315
  1.8 15.2 %collective-permute-start.5 = (f32[2,128,128]{2,1,0:T(8,128)S(1)}, f32[2,128,128]{2,1,0:T(8,128)S(1)}, u32[]{:S(2)}, u32[]{:S(2)}) collective-permute-start(f32[2,128,128]{2,1,0:T(8,128)S(1)} %get-tuple-element.34), channel_id=1, source_target_pairs={{0,10},{1,11},{2,8},{3,9},{4,14},{5,15},{6,12},{7,13},{8,18},{9,19... | collective-permute-start | bytes 393224 | tf_op jit(solution)/shard_map/ppermute | solution.py:315
  4.4 5.5 %collective-permute-start.3 = (f32[2,128,128]{2,1,0:T(8,128)S(1)}, f32[2,128,128]{2,1,0:T(8,128)S(1)}, u32[]{:S(2)}, u32[]{:S(2)}) collective-permute-start(f32[2,128,128]{2,1,0:T(8,128)S(1)} %get-tuple-element.33), channel_id=1, source_target_pairs={{0,4},{1,5},{2,6},{3,7},{4,0},{5,1},{6,2},{7,3},{8,12},{9,13},{10,... | collective-permute-start | bytes 393224 | tf_op jit(solution)/shard_map/ppermute | solution.py:315
  6.0 10.5 %collective-permute-start.4 = (f32[2,128,128]{2,1,0:T(8,128)S(1)}, f32[2,128,128]{2,1,0:T(8,128)S(1)}, u32[]{:S(2)}, u32[]{:S(2)}) collective-permute-start(f32[2,128,128]{2,1,0:T(8,128)S(1)} %get-tuple-element.35.refs_0_), channel_id=1, source_target_pairs={{0,8},{1,9},{2,10},{3,11},{4,12},{5,13},{6,14},{7,15},{8,16},{9,17... | collective-permute-start | bytes 393224 | tf_op jit(solution)/shard_map/ppermute | solution.py:315
  7.5 5.5 %collective-permute-start = (f32[2,128,128]{2,1,0:T(8,128)S(1)}, f32[2,128,128]{2,1,0:T(8,128)S(1)}, u32[]{:S(2)}, u32[]{:S(2)}) collective-permute-start(f32[2,128,128]{2,1,0:T(8,128)S(1)} %get-tuple-element.36), channel_id=1, source_target_pairs={{0,6},{1,7},{2,4},{3,5},{4,2},{5,3},{6,0},{7,1},{8,14},{9,15},{10,... | collective-permute-start | bytes 393224 | tf_op jit(solution)/shard_map/ppermute | solution.py:315
  9.9 9.1 %collective-permute-start.6 = (f32[2,128,128]{2,1,0:T(8,128)S(1)}, f32[2,128,128]{2,1,0:T(8,128)S(1)}, u32[]{:S(2)}, u32[]{:S(2)}) collective-permute-start(f32[2,128,128]{2,1,0:T(8,128)S(1)} %collective-permute-done.3.refs_2_), channel_id=1, source_target_pairs={{0,8},{1,9},{2,10},{3,11},{4,12},{5,13},{6,14},{7,15},{8,16},{9,17... | collective-permute-start | bytes 393224 | tf_op jit(solution)/shard_map/ppermute | solution.py:315
  13.0 7.2 %collective-permute-start.1 = (f32[2,128,128]{2,1,0:T(8,128)S(1)}, f32[2,128,128]{2,1,0:T(8,128)S(1)}, u32[]{:S(2)}, u32[]{:S(2)}) collective-permute-start(f32[2,128,128]{2,1,0:T(8,128)S(1)} %collective-permute-done.piece), channel_id=1, source_target_pairs={{0,8},{1,9},{2,10},{3,11},{4,12},{5,13},{6,14},{7,15},{8,16},{9,17... | collective-permute-start | bytes 393224 | tf_op jit(solution)/shard_map/ppermute | solution.py:315
  19.0 1.2 %copy-start.2 = (bf16[1024,256]{1,0:T(8,128)(2,1)S(1)}, bf16[1024,256]{1,0:T(8,128)(2,1)}, u32[]{:S(2)}) copy-start(bf16[1024,256]{1,0:T(8,128)(2,1)} %constant.79.clone.t_high) | copy-start | bytes 1572868
  19.0 1.2 %copy-start.3 = (bf16[1024,256]{1,0:T(8,128)(2,1)S(1)}, bf16[1024,256]{1,0:T(8,128)(2,1)}, u32[]{:S(2)}) copy-start(bf16[1024,256]{1,0:T(8,128)(2,1)} %constant.80.clone.t_low) | copy-start | bytes 1572868
  21.8 1.6 %collective-permute-start.9 = (f32[2,32,128]{2,1,0:T(8,128)S(1)}, f32[2,32,128]{2,1,0:T(8,128)S(1)}, u32[]{:S(2)}, u32[]{:S(2)}) collective-permute-start(f32[2,32,128]{2,1,0:T(8,128)S(1)} %get-tuple-element.29), channel_id=1, source_target_pairs={{0,2},{1,3},{2,0},{3,1},{4,6},{5,7},{6,4},{7,5},{8,10},{9,11},{10,... | collective-permute-start | bytes 98312 | tf_op jit(solution)/shard_map/ppermute | solution.py:315
  22.9 3.6 %collective-permute-start.7 = (f32[2,32,128]{2,1,0:T(8,128)S(1)}, f32[2,32,128]{2,1,0:T(8,128)S(1)}, u32[]{:S(2)}, u32[]{:S(2)}) collective-permute-start(f32[2,32,128]{2,1,0:T(8,128)S(1)} %get-tuple-element.26), channel_id=1, source_target_pairs={{0,2},{1,3},{2,0},{3,1},{4,6},{5,7},{6,4},{7,5},{8,10},{9,11},{10,... | collective-permute-start | bytes 98312 | tf_op jit(solution)/shard_map/ppermute | solution.py:315
  23.4 4.9 %collective-permute-start.11 = (f32[2,32,128]{2,1,0:T(8,128)S(1)}, f32[2,32,128]{2,1,0:T(8,128)S(1)}, u32[]{:S(2)}, u32[]{:S(2)}) collective-permute-start(f32[2,32,128]{2,1,0:T(8,128)S(1)} %pad_maximum_fusion.2), channel_id=1, source_target_pairs={{0,5},{1,4},{2,7},{3,6},{4,1},{5,0},{6,3},{7,2},{8,13},{9,12},{10,... | collective-permute-start | bytes 98312 | tf_op jit(solution)/shard_map/ppermute | solution.py:315
  25.7 3.9 %collective-permute-start.10 = (f32[2,32,128]{2,1,0:T(8,128)S(1)}, f32[2,32,128]{2,1,0:T(8,128)S(1)}, u32[]{:S(2)}, u32[]{:S(2)}) collective-permute-start(f32[2,32,128]{2,1,0:T(8,128)S(1)} %pad_maximum_fusion.1), channel_id=1, source_target_pairs={{0,4},{1,5},{2,6},{3,7},{4,0},{5,1},{6,2},{7,3},{8,12},{9,13},{10,... | collective-permute-start | bytes 98312 | tf_op jit(solution)/shard_map/ppermute | solution.py:315
  26.5 4.0 %collective-permute-start.8 = (f32[2,32,128]{2,1,0:T(8,128)S(1)}, f32[2,32,128]{2,1,0:T(8,128)S(1)}, u32[]{:S(2)}, u32[]{:S(2)}) collective-permute-start(f32[2,32,128]{2,1,0:T(8,128)S(1)} %pad_maximum_fusion), channel_id=1, source_target_pairs={{0,1},{1,0},{2,3},{3,2},{4,5},{5,4},{6,7},{7,6},{8,9},{9,8},{10,11... | collective-permute-start | bytes 98312 | tf_op jit(solution)/shard_map/ppermute | solution.py:315
where the time goes:
time: 32 us; the launch traced here: 31.8 us
  starting transfers between devices  13.7 us (43%)
  Pallas kernels  9.3 us (29%)
  waiting for transfers between devices  6.65 us (21%)
  local copies, waits for them, and re-layouts  1.43 us (4%)
  other arithmetic  0.52 us (2%)
    ppermute x12, starting transfers between devices, move(): return lax.ppermute(value, ('rx', 'tm'), pairs)  13.7 us
    ppermute x12, waiting for transfers between devices, move(): return lax.ppermute(value, ('rx', 'tm'), pairs)  6.65 us
    pallas_call x1, Pallas kernels, per_device(): pl.pallas_call(functools.partial(own_kernel, segs), out_shape=(spectra, s...  1.76 us
    pallas_call x1, Pallas kernels, per_device(): pl.pallas_call(functools.partial(level_kernel, segs), out_shape=(spectra,...  1.61 us
    pallas_call x1, Pallas kernels, per_device(): pl.pallas_call(functools.partial(first_kernel, segs, parts), out_shape=(s...  1.59 us
    pallas_call x1, Pallas kernels, per_device(): pl.pallas_call(functools.partial(doppler_kernel, segs), out_shape=jax.Sha...  1.36 us
    dynamic_slice x1, local copies, waits for them, and re-layouts, per_device(): lax.dynamic_slice_in_dim(raw, (me ^ slot) * (segs * ROWS), segs * ROWS, a...  1.19 us
    pallas_call x1, Pallas kernels, per_device(): pl.pallas_call(functools.partial(ahead_kernel, segs, last - 1), out_shape...  1.15 us
  transfers between devices with their start and end apart: 12, of which 5 were waited for; matrix products, arithmetic and copies ran while one was open for 2% of the time, Pallas kernels for 20%

commit v1 on v0

--- a/solution.py
+++ b/solution.py
@@ -21,11 +21,11 @@
 WINDOW = 2 * LAGS
 BLOCKS = SEG_LEN // BLOCK
 ROWS = SEG_LEN // HALF
+CLASSES = 4
+WIDE = WINDOW // CLASSES * 2
 STORES = 4
 
 VMEM = pl.BlockSpec(memory_space=pltpu.VMEM)
-SMEM = pl.BlockSpec(memory_space=pltpu.SMEM)
-HBM = pl.BlockSpec(memory_space=pltpu.HBM)
 ANY = pl.BlockSpec(memory_space=pl.ANY)
 
 
@@ -41,9 +41,22 @@
     return jnp.asarray(high), jnp.asarray((table - high.astype(np.float64)).astype(jnp.bfloat16))
 
 
-def trig(rows, columns):
-    angle = 2.0 * math.pi / WINDOW * (np.outer(rows, columns) % WINDOW)
-    return np.concatenate([np.cos(angle), np.sin(angle)], axis=0)
+def forward_table():
+    blocks = []
+    for first in range(CLASSES):
+        turns = np.outer(np.arange(HALF), np.arange(first, WINDOW, CLASSES)) % WINDOW
+        cos, sin = np.cos(2.0 * math.pi / WINDOW * turns), np.sin(2.0 * math.pi / WINDOW * turns)
+        blocks.append(np.block([[cos, -sin], [sin, cos]]))
+    return np.concatenate(blocks, axis=0)
+
+
+def inverse_table():
+    blocks = []
+    for first in range(CLASSES):
+        turns = np.outer(np.arange(first, WINDOW, CLASSES), np.arange(HALF)) % WINDOW
+        cos, sin = np.cos(2.0 * math.pi / WINDOW * turns), np.sin(2.0 * math.pi / WINDOW * turns)
+        blocks.append(np.block([[cos, sin], [-sin, cos]]) / WINDOW)
+    return np.concatenate(blocks, axis=0)
 
 
 def split(value):
@@ -78,12 +91,35 @@
                 ]
 
 
-def transform(scratch, table_high, table_low):
-    straight = scratch[...]
-    count = straight.shape[0]
-    crossed = jnp.concatenate([straight[:, BLOCK:], -straight[:, :BLOCK]], axis=1)
-    out = product(jnp.concatenate([straight, crossed], axis=0), table_high[...], table_low[...])
-    return out[:count], out[count:]
+def add_turned(total, value, power):
+    (a, b), (c, d) = total, value
+    return ((a + c, b + d), (a + d, b - c), (a - c, b - d), (a - d, b + c))[power % 4]
+
+
+def table_block(table_ref, kind):
+    return table_ref[kind * WIDE : (kind + 1) * WIDE, :]
+
+
+def transform(scratch, table_high, table_low, store, count, whole):
+    def part(first, place):
+        rows = slice(first, first + count)
+        real, imag = place * HALF, BLOCK + place * HALF
+        return scratch[rows, real : real + HALF], scratch[rows, imag : imag + HALF]
+
+    odd, even = part(0, 0), part(0, 1)
+    for kind in range(CLASSES):
+        value = add_turned(odd, even, kind)
+        left = jnp.concatenate(value, axis=1)
+        if whole:
+            value = add_turned(value, part(count, 1), -kind)
+            value = add_turned(value, part(count, 0), 2 * kind)
+            left = jnp.concatenate([left, jnp.concatenate(value, axis=1)], axis=0)
+        out = product(left, table_block(table_high, kind), table_block(table_low, kind))
+        store(pl.ds(kind * WIDE, WIDE), out)
+
+
+def position(parts):
+    return lax.rem(lax.axis_index("rx"), OFFS), lax.axis_index("tm") if parts > 1 else 0
 
 
 def swap_halves(value):
@@ -95,9 +131,9 @@
     for row in range(0, x_ref.shape[1], tile):
         rows = pl.ds(row, tile)
         x_re = x_ref[x_slot, rows, pl.ds(column, HALF)]
-        x_im = x_ref[x_slot, rows, pl.ds(WINDOW + column, HALF)]
+        x_im = x_ref[x_slot, rows, pl.ds(column + HALF, HALF)]
         y_re = y_ref[y_slot, rows, pl.ds(column, HALF)]
-        y_im = y_ref[y_slot, rows, pl.ds(WINDOW + column, HALF)]
+        y_im = y_ref[y_slot, rows, pl.ds(column + HALF, HALF)]
         more_re = x_re * y_re + x_im * y_im
         more_im = x_im * y_re - x_re * y_im
         re, im = (more_re, more_im) if re is None else (re + more_re, im + more_im)
@@ -109,7 +145,7 @@
     first_half = lax.broadcasted_iota(jnp.int32, (tile, HALF), 0) < segs
     zero = jnp.zeros((tile, HALF), jnp.float32)
     for q in range(OFFS):
-        for column in range(0, WINDOW, HALF):
+        for column in range(0, 2 * WINDOW, WIDE):
             sums = [
                 pair_sum(x_ref, q ^ me, y_ref, (q - 1 - o) ^ me, column, tile)
                 if o < q
@@ -118,7 +154,7 @@
             ]
             for o in range(0, OFFS, 2):
                 rows = pl.ds((q * OFFS + o) * segs, tile)
-                for part, base in ((0, 0), (1, WINDOW)):
+                for part, base in ((0, 0), (1, HALF)):
                     a, b = sums[o][part], sums[o + 1][part]
                     spectrum[rows, pl.ds(base + column, HALF)] = jnp.where(
                         first_half, a, b
@@ -134,9 +170,9 @@
         second = lax.broadcasted_iota(jnp.int32, (tile, HALF), 0) >= segs
         mine = second == (lax.rem(o, 2) == 1)
         rows = pl.ds(pl.multiple_of(first_row + (o - lax.rem(o, 2)) * segs, tile), tile)
-        for column in range(0, WINDOW, HALF):
+        for column in range(0, 2 * WINDOW, WIDE):
             sums = pair_sum(x_ref, x_slot, y_ref, 0, column, tile)
-            for value, base in zip(sums, (0, WINDOW)):
+            for value, base in zip(sums, (0, HALF)):
                 columns = pl.ds(base + column, HALF)
                 total = value + swap_halves(value)
                 spectrum[rows, columns] = spectrum[rows, columns] + jnp.where(mine, total, 0.0)
@@ -144,14 +180,14 @@
 
 def own_transform(piece, slot, table_high, table_low, x_out, y_out, scratch, segs):
     rows = BLOCKS * segs
-    odd = lax.broadcasted_iota(jnp.int32, (rows, WINDOW), 1) % 2 == 1
     gather_rows(piece, scratch, 0, (1, 2), segs)
     gather_rows(piece, scratch, rows, (3, 0), segs)
-    re, im = transform(scratch, table_high, table_low)
-    y_out[slot, :, :WINDOW] = re[:rows]
-    y_out[slot, :, WINDOW:] = im[:rows]
-    x_out[slot, :, :WINDOW] = re[:rows] + jnp.where(odd, -re[rows:], re[rows:])
-    x_out[slot, :, WINDOW:] = im[:rows] + jnp.where(odd, -im[rows:], im[rows:])
+
+    def store(columns, value):
+        y_out[slot, :, columns] = value[:rows]
+        x_out[slot, :, columns] = value[rows:]
+
+    transform(scratch, table_high, table_low, store, rows, True)
 
 
 def own_kernel(segs, *refs):
@@ -162,19 +198,21 @@
 
 def far_transform(piece, table_high, table_low, y_out, scratch, segs):
     gather_rows(piece, scratch, 0, (1, 2), segs)
-    y_re, y_im = transform(scratch, table_high, table_low)
-    y_out[0, :, :WINDOW] = y_re
-    y_out[0, :, WINDOW:] = y_im
+
+    def store(columns, value):
+        y_out[0, :, columns] = value
+
+    transform(scratch, table_high, table_low, store, BLOCKS * segs, False)
 
 
 def far_kernel(segs, piece, table_high, table_low, y_out, scratch):
     far_transform(piece, table_high, table_low, y_out, scratch, segs)
 
 
-def level_kernel(segs, place, piece, table_high, table_low, x_in, y_in, *refs):
+def level_kernel(segs, piece, table_high, table_low, x_in, y_in, *refs):
     del x_in, y_in
     ready, (x_out, y_out, spectrum, scratch) = refs[:-4], refs[-4:]
-    me = place[0]
+    me, _ = position(1)
     own_transform(piece, OFFS - 1, table_high, table_low, x_out, y_out, scratch, segs)
     near_pairs(segs, me, x_out, y_out, spectrum)
     for slot, y_ref in enumerate(ready):
@@ -184,17 +222,17 @@
 
 
 def ahead_kernel(
-    segs, slot, place, piece, table_high, table_low, x_ref, _, spectrum, y_scratch, scratch
+    segs, slot, piece, table_high, table_low, x_ref, _, spectrum, y_scratch, scratch
 ):
     far_transform(piece, table_high, table_low, y_scratch, scratch, segs)
-    me = place[0]
+    me, _ = position(1)
     for x_slot in range(OFFS):
         q = me ^ x_slot
         far_pair(segs, q, me ^ slot, x_ref, x_slot, y_scratch, spectrum, q * (OFFS * segs))
 
 
-def finish(segs, parts, dy, place, x_ref, y_ref, sums, t_high, t_low, outs, spectrum, held):
-    me, my_part = place[0], place[1]
+def finish(segs, parts, dy, x_ref, y_ref, sums, t_high, t_low, outs, spectrum, held):
+    me, my_part = position(parts)
     tile = 2 * segs
     lag_dev = LAGS // parts
     count = OFFS * segs
@@ -205,17 +243,23 @@
             pl.ds(pl.multiple_of(q * count, count), count), :
         ]
         far_pair(segs, q, me ^ (OFFS - 1), x_ref, x_slot, y_ref, spectrum, index * count)
-    s_re, s_im = spectrum[:, :WINDOW], spectrum[:, WINDOW:]
-    left = jnp.concatenate(
-        [jnp.concatenate([s_re, -s_im], axis=1), jnp.concatenate([s_im, s_re], axis=1)], axis=0
-    )
-    corr = product(left, t_high[...], t_low[...])
+    early, late = None, None
+    for kind in range(CLASSES):
+        out = product(
+            spectrum[:, kind * WIDE : (kind + 1) * WIDE],
+            table_block(t_high, kind),
+            table_block(t_low, kind),
+        )
+        value = (out[:, :HALF], out[:, HALF:])
+        early = add_turned(early, value, kind) if early else value
+        late = add_turned(late, value, 0) if late else value
+    corr_re = jnp.concatenate([early[0], late[0]], axis=1)
+    corr_im = jnp.concatenate([early[1], late[1]], axis=1)
     wide_half = lax.broadcasted_iota(jnp.int32, (tile, LAGS), 0) < segs
     for index in range(len(slots)):
         for o in range(0, OFFS, 2):
             row = (index * OFFS + o) * segs
-            re = corr[row : row + tile]
-            im = corr[len(slots) * count + row : len(slots) * count + row + tile]
+            re, im = corr_re[row : row + tile], corr_im[row : row + tile]
             first = jnp.where(wide_half, re, swap_halves(im))
             second = jnp.where(wide_half, swap_halves(re), im)
             for t in range(parts):
@@ -229,15 +273,15 @@
         send[dt] = held[parts + there]
 
 
-def first_kernel(segs, parts, place, piece, table_high, table_low, x_ref, sums, t_high, t_low, *refs):
+def first_kernel(segs, parts, piece, table_high, table_low, x_ref, sums, t_high, t_low, *refs):
     (y_out, *outs), (scratch, spectrum, held) = refs[:-3], refs[-3:]
     far_transform(piece, table_high, table_low, y_out, scratch, segs)
-    finish(segs, parts, 1, place, x_ref, y_out, sums, t_high, t_low, outs, spectrum, held)
-
-
-def second_kernel(segs, parts, place, y_ref, x_ref, sums, t_high, t_low, *refs):
+    finish(segs, parts, 1, x_ref, y_out, sums, t_high, t_low, outs, spectrum, held)
+
+
+def second_kernel(segs, parts, y_ref, x_ref, sums, t_high, t_low, *refs):
     outs, (spectrum, held) = refs[:-2], refs[-2:]
-    finish(segs, parts, 0, place, x_ref, y_ref, sums, t_high, t_low, outs, spectrum, held)
+    finish(segs, parts, 0, x_ref, y_ref, sums, t_high, t_low, outs, spectrum, held)
 
 
 def doppler_kernel(segs, keep_ref, recv_ref, *refs):
@@ -304,7 +348,6 @@
     assert rec_dev == 1 and count % OFFS == 0 and seg_dev % OFFS == 0
     me = lax.axis_index("rx") % OFFS
     my_part = lax.axis_index("tm")
-    place = jnp.stack([me, my_part]).astype(jnp.int32)
 
     def move(value, flip, ahead=0, later=0):
         pairs = []
@@ -329,9 +372,8 @@
         for slot in range(OFFS)
     ]
 
-    frequency = np.arange(WINDOW)
-    high, low = halves(trig(np.arange(BLOCK), frequency))
-    t_high, t_low = halves(trig(frequency, np.arange(LAGS) - HALF) / WINDOW)
+    high, low = halves(forward_table())
+    t_high, t_low = halves(inverse_table())
 
     rows = BLOCKS * segs
     last = OFFS - 1
@@ -364,23 +406,23 @@
     x_own, _, total = pl.pallas_call(
         functools.partial(level_kernel, segs),
         out_shape=(spectra, spectra, sums),
-        in_specs=[SMEM] + [VMEM] * (5 + len(ready)),
+        in_specs=[VMEM] * (5 + len(ready)),
         out_specs=(VMEM, VMEM, VMEM),
         scratch_shapes=[own_rows],
-        input_output_aliases={4: 0, 5: 1},
+        input_output_aliases={3: 0, 4: 1},
         compiler_params=limit(6),
         name="level",
-    )(place, own[last], high, low, x_own, y_own, *ready)
+    )(own[last], high, low, x_own, y_own, *ready)
     total = pl.pallas_call(
         functools.partial(ahead_kernel, segs, last - 1),
         out_shape=sums,
-        in_specs=[SMEM] + [VMEM] * 5,
+        in_specs=[VMEM] * 5,
         out_specs=VMEM,
         scratch_shapes=[pltpu.VMEM(spectrum.shape, jnp.float32), far_rows],
-        input_output_aliases={5: 0},
+        input_output_aliases={4: 0},
         compiler_params=limit(4),
         name="ahead",
-    )(place, far[last - 1], high, low, x_own, total)
+    )(far[last - 1], high, low, x_own, total)
 
     lag_dev = LAGS // parts
     piece_rows = OFFS * 2 * segs
@@ -402,21 +444,21 @@
     y_last, *crossing = pl.pallas_call(
         functools.partial(first_kernel, segs, parts),
         out_shape=(spectrum, *leaving),
-        in_specs=[SMEM] + [VMEM] * 7,
+        in_specs=[VMEM] * 7,
         out_specs=(VMEM,) * (2 + parts),
         scratch_shapes=[far_rows] + working,
         compiler_params=limit(6),
         name="first",
-    )(place, far[last], high, low, x_own, total, t_high, t_low)
+    )(far[last], high, low, x_own, total, t_high, t_low)
     staying = pl.pallas_call(
         functools.partial(second_kernel, segs, parts),
         out_shape=leaving,
-        in_specs=[SMEM] + [VMEM] * 5,
+        in_specs=[VMEM] * 5,
         out_specs=(VMEM,) * (1 + parts),
         scratch_shapes=working,
         compiler_params=limit(6),
         name="second",
-    )(place, y_last, x_own, total, t_high, t_low)
+    )(y_last, x_own, total, t_high, t_low)
     got = {1: move(crossing[0], 1), 0: move(staying[0], 1)}
     kept = {1: crossing[1:], 0: staying[1:]}
     keep, recv = kept[0][0], got[0]

time: 32 us -> 30.6 us (0.956)
  Pallas kernels: 9.3 us -> 5.96 us
  waiting for transfers between devices: 6.65 us -> 8.68 us
    ppermute x12, waiting for transfers between devices: 6.65 us -> 8.68 us  [move(): return lax.ppermute(value, ('rx', 'tm'), pairs)]
    pallas_call x1, Pallas kernels: 1.59 us -> 0.73 us  [per_device(): pl.pallas_call(functools.partial(first_kernel, segs, parts), out_shape=(s...]
    pallas_call x1, Pallas kernels: 1.61 us -> 0.94 us  [per_device(): pl.pallas_call(functools.partial(level_kernel, segs), out_shape=(spectra,...]
    pallas_call x1, Pallas kernels: 1.15 us -> 0.52 us  [per_device(): pl.pallas_call(functools.partial(ahead_kernel, segs, last - 1), out_shape...]
    pallas_call x1, Pallas kernels: 0.98 us -> 0.41 us  [per_device(): pl.pallas_call(functools.partial(second_kernel, segs, parts), out_shape=l...]
    pallas_call x1, Pallas kernels: 1.76 us -> 1.24 us  [per_device(): pl.pallas_call(functools.partial(own_kernel, segs), out_shape=(spectra, s...]
  transfers between devices with their start and end apart: 12 -> 12, of which waited for: 5 -> 7; matrix products, arithmetic and copies ran while one was open for 2% -> 2% of each run, Pallas kernels for 20% -> 13%
where the time goes in v1:
time: 30.6 us; the launch traced here: 30.4 us
  starting transfers between devices  13.7 us (45%)
  waiting for transfers between devices  8.68 us (28%)
  Pallas kernels  5.96 us (19%)
  local copies, waits for them, and re-layouts  1.43 us (5%)
  other arithmetic  0.44 us (1%)
    ppermute x12, starting transfers between devices, move(): return lax.ppermute(value, ('rx', 'tm'), pairs)  13.7 us
    ppermute x12, waiting for transfers between devices, move(): return lax.ppermute(value, ('rx', 'tm'), pairs)  8.68 us
    pallas_call x1, Pallas kernels, per_device(): pl.pallas_call(functools.partial(doppler_kernel, segs), out_shape=jax.Sha...  1.36 us
    pallas_call x1, Pallas kernels, per_device(): pl.pallas_call(functools.partial(own_kernel, segs), out_shape=(spectra, s...  1.24 us
    dynamic_slice x1, local copies, waits for them, and re-layouts, per_device(): lax.dynamic_slice_in_dim(raw, (me ^ slot) * (segs * ROWS), segs * ROWS, a...  1.19 us
    pallas_call x1, Pallas kernels, per_device(): pl.pallas_call(functools.partial(level_kernel, segs), out_shape=(spectra,...  0.94 us
    pallas_call x2, Pallas kernels, per_device(): pl.pallas_call(functools.partial(far_kernel, segs), out_shape=spectrum, i...  0.76 us
    pallas_call x1, Pallas kernels, per_device(): pl.pallas_call(functools.partial(first_kernel, segs, parts), out_shape=(s...  0.73 us
  transfers between devices with their start and end apart: 12, of which 7 were waited for; matrix products, arithmetic and copies ran while one was open for 2% of the time, Pallas kernels for 13%

profile of v1, /device:TPU:0, one launch (start us, length us, event | category | flops | bytes accessed | tf_op | source)
XLA Modules:
  0.0 30.4 jit_solution(9657706205209293792)
XLA Ops:
  0.0 1.2 %constant_dynamic-slice_fusion = (f32[2,128,128]{2,1,0:T(8,128)S(1)}, f32[2,128,128]{2,1,0:T(8,128)S(1)}, f32[2,128,128]{2,1,0:T(8,128)S(1)}, f32[2,128,128]{2,1,0:T(8,128)S(1)}) fusion(f32[2,512,128]{2,1,0:T(8,128)} %bitcast.8, s32[]{:T(128)S(6)} %select_n.57, s32[]{:T(128)S(6)} %select_n.56, s32[]{:T(128)S(6)} %select_n.55, s32[]{:T(128)S(6)} %select_n.54), kind=kLoop, calls=%fused_computation.19 | loop fusion | bytes 1048592 | tf_op jit(solution)/shard_map/dynamic_slice | solution.py:363
  1.2 0.6 %collective-permute-start.2 = (f32[2,128,128]{2,1,0:T(8,128)S(1)}, f32[2,128,128]{2,1,0:T(8,128)S(1)}, u32[]{:S(2)}, u32[]{:S(2)}) collective-permute-start(f32[2,128,128]{2,1,0:T(8,128)S(1)} %get-tuple-element.34), channel_id=1, source_target_pairs={{0,2},{1,3},{2,0},{3,1},{4,6},{5,7},{6,4},{7,5},{8,10},{9,11},{10,... | collective-permute-start | bytes 393224 | tf_op jit(solution)/shard_map/ppermute | solution.py:358
  1.8 2.7 %collective-permute-start.5 = (f32[2,128,128]{2,1,0:T(8,128)S(1)}, f32[2,128,128]{2,1,0:T(8,128)S(1)}, u32[]{:S(2)}, u32[]{:S(2)}) collective-permute-start(f32[2,128,128]{2,1,0:T(8,128)S(1)} %get-tuple-element.34), channel_id=1, source_target_pairs={{0,10},{1,11},{2,8},{3,9},{4,14},{5,15},{6,12},{7,13},{8,18},{9,19... | collective-permute-start | bytes 393224 | tf_op jit(solution)/shard_map/ppermute | solution.py:358
  4.4 1.5 %collective-permute-start.3 = (f32[2,128,128]{2,1,0:T(8,128)S(1)}, f32[2,128,128]{2,1,0:T(8,128)S(1)}, u32[]{:S(2)}, u32[]{:S(2)}) collective-permute-start(f32[2,128,128]{2,1,0:T(8,128)S(1)} %get-tuple-element.33), channel_id=1, source_target_pairs={{0,4},{1,5},{2,6},{3,7},{4,0},{5,1},{6,2},{7,3},{8,12},{9,13},{10,... | collective-permute-start | bytes 393224 | tf_op jit(solution)/shard_map/ppermute | solution.py:358
  6.0 1.6 %collective-permute-start.4 = (f32[2,128,128]{2,1,0:T(8,128)S(1)}, f32[2,128,128]{2,1,0:T(8,128)S(1)}, u32[]{:S(2)}, u32[]{:S(2)}) collective-permute-start(f32[2,128,128]{2,1,0:T(8,128)S(1)} %get-tuple-element.35.refs_0_), channel_id=1, source_target_pairs={{0,8},{1,9},{2,10},{3,11},{4,12},{5,13},{6,14},{7,15},{8,16},{9,17... | collective-permute-start | bytes 393224 | tf_op jit(solution)/shard_map/ppermute | solution.py:358
  8.2 1.7 %collective-permute-done.3.refs_2_ = f32[2,128,128]{2,1,0:T(8,128)S(1)} collective-permute-done((f32[2,128,128]{2,1,0:T(8,128)S(1)}, f32[2,128,128]{2,1,0:T(8,128)S(1)}, u32[]{:S(2)}, u32[]{:S(2)}) %collective-permute-start.3) | collective-permute-done | bytes 131104 | tf_op jit(solution)/shard_map/ppermute | solution.py:358
  9.9 1.6 %collective-permute-start.6 = (f32[2,128,128]{2,1,0:T(8,128)S(1)}, f32[2,128,128]{2,1,0:T(8,128)S(1)}, u32[]{:S(2)}, u32[]{:S(2)}) collective-permute-start(f32[2,128,128]{2,1,0:T(8,128)S(1)} %collective-permute-done.3.refs_2_), channel_id=1, source_target_pairs={{0,8},{1,9},{2,10},{3,11},{4,12},{5,13},{6,14},{7,15},{8,16},{9,17... | collective-permute-start | bytes 393224 | tf_op jit(solution)/shard_map/ppermute | solution.py:358
  11.5 1.5 %collective-permute-done.piece = f32[2,128,128]{2,1,0:T(8,128)S(1)} collective-permute-done((f32[2,128,128]{2,1,0:T(8,128)S(1)}, f32[2,128,128]{2,1,0:T(8,128)S(1)}, u32[]{:S(2)}, u32[]{:S(2)}) %collective-permute-start) | collective-permute-done | bytes 131104 | tf_op jit(solution)/shard_map/ppermute | solution.py:358
  13.0 1.6 %collective-permute-start.1 = (f32[2,128,128]{2,1,0:T(8,128)S(1)}, f32[2,128,128]{2,1,0:T(8,128)S(1)}, u32[]{:S(2)}, u32[]{:S(2)}) collective-permute-start(f32[2,128,128]{2,1,0:T(8,128)S(1)} %collective-permute-done.piece), channel_id=1, source_target_pairs={{0,8},{1,9},{2,10},{3,11},{4,12},{5,13},{6,14},{7,15},{8,16},{9,17... | collective-permute-start | bytes 393224 | tf_op jit(solution)/shard_map/ppermute | solution.py:358
  14.7 1.2 %own.1 = (f32[4,64,1024]{2,1,0:T(8,128)S(1)}, f32[4,64,1024]{2,1,0:T(8,128)S(1)}) custom-call(f32[2,128,128]{2,1,0:T(8,128)S(1)} %get-tuple-element.35.refs_0_, f32[2,128,128]{2,1,0:T(8,128)S(1)} %collective-permute-done.2.refs_1_, f32[2,128,128]{2,1,0:T(8,128)S(1)} %collective-permute-done.3.refs_2_, bf16[1024,256]{1,0:T(8,128)(2,1)S(1)} %copy-done, ...), custom_call_target="tpu_custom_call" | custom-call | tf_op jit(solution)/shard_map/own/pallas_call | solution.py:385
  15.9 0.4 %far.2.refs_0_ = f32[1,64,1024]{2,1,0:T(8,128)S(1)} custom-call(f32[2,128,128]{2,1,0:T(8,128)S(1)} %collective-permute-done.4.piece, bf16[1024,256]{1,0:T(8,128)(2,1)S(1)} %copy-done, bf16[1024,256]{1,0:T(8,128)(2,1)S(1)} %copy-done.1), custom_call_target="tpu_custom_call" | custom-call | tf_op jit(solution)/shard_map/far/pallas_call | solution.py:395
  16.7 0.9 %level.1 = (f32[4,64,1024]{2,1,0:T(8,128)S(1)}, f32[4,64,1024]{2,1,0:T(8,128)S(1)}, f32[64,1024]{1,0:T(8,128)S(1)}) custom-call(f32[2,128,128]{2,1,0:T(8,128)S(1)} %collective-permute-done.piece, bf16[1024,256]{1,0:T(8,128)(2,1)S(1)} %copy-done, bf16[1024,256]{1,0:T(8,128)(2,1)S(1)} %copy-done.1, ...), custom_call_target="tpu_custom_call", output_to_operand_aliasing={{0}: (3, {}), {1}: (4, {})} | custom-call | tf_op jit(solution)/shard_map/level/pallas_call | solution.py:406
  17.7 0.5 %ahead.1.sums = f32[64,1024]{1,0:T(8,128)S(1)} custom-call(f32[2,128,128]{2,1,0:T(8,128)S(1)} %collective-permute-done.6.piece, bf16[1024,256]{1,0:T(8,128)(2,1)S(1)} %copy-done, bf16[1024,256]{1,0:T(8,128)(2,1)S(1)} %copy-done.1, f32[4,64,1024]{2,1,0:T(8,128)S(1)} %get-tuple-element.21.x_ref, ...), custom_call_target="tpu_custom_call", output_to_operand_aliasing={{}: (4, {})} | custom-call | tf_op jit(solution)/shard_map/ahead/pallas_call | solution.py:416
  18.2 1.8 %collective-permute-done.1.piece = f32[2,128,128]{2,1,0:T(8,128)S(1)} collective-permute-done((f32[2,128,128]{2,1,0:T(8,128)S(1)}, f32[2,128,128]{2,1,0:T(8,128)S(1)}, u32[]{:S(2)}, u32[]{:S(2)}) %collective-permute-start.1) | collective-permute-done | bytes 131104 | tf_op jit(solution)/shard_map/ppermute | solution.py:358
  20.0 0.7 %first.1 = (f32[1,64,1024]{2,1,0:T(8,128)S(1)}, f32[2,32,128]{2,1,0:T(8,128)S(1)}, f32[32,128]{1,0:T(8,128)S(1)}, f32[32,128]{1,0:T(8,128)S(1)}) custom-call(f32[2,128,128]{2,1,0:T(8,128)S(1)} %collective-permute-done.1.piece, bf16[1024,256]{1,0:T(8,128)(2,1)S(1)} %copy-done, bf16[1024,256]{1,0:T(8,128)(2,1)S(1)} %copy-done.1, ...), custom_call_target="tpu_custom_call" | custom-call | tf_op jit(solution)/shard_map/first/pallas_call | solution.py:444
  20.8 0.4 %second.1 = (f32[2,32,128]{2,1,0:T(8,128)S(1)}, f32[32,128]{1,0:T(8,128)S(1)}, f32[32,128]{1,0:T(8,128)S(1)}) custom-call(f32[1,64,1024]{2,1,0:T(8,128)S(1)} %get-tuple-element.24.y_ref, f32[4,64,1024]{2,1,0:T(8,128)S(1)} %get-tuple-element.21.x_ref, f32[64,1024]{1,0:T(8,128)S(1)} %ahead.1.sums, bf16[1024,256]{1,0:T(8,128)(2,1)S(1)} %copy-done.2, ...), custom_call_target="tpu_custom_call" | custom-call | tf_op jit(solution)/shard_map/second/pallas_call | solution.py:453
  21.3 0.5 %collective-permute-start.7 = (f32[2,32,128]{2,1,0:T(8,128)S(1)}, f32[2,32,128]{2,1,0:T(8,128)S(1)}, u32[]{:S(2)}, u32[]{:S(2)}) collective-permute-start(f32[2,32,128]{2,1,0:T(8,128)S(1)} %get-tuple-element.26), channel_id=1, source_target_pairs={{0,2},{1,3},{2,0},{3,1},{4,6},{5,7},{6,4},{7,5},{8,10},{9,11},{10,... | collective-permute-start | bytes 98312 | tf_op jit(solution)/shard_map/ppermute | solution.py:358
  22.0 2.5 %collective-permute-start.11 = (f32[2,32,128]{2,1,0:T(8,128)S(1)}, f32[2,32,128]{2,1,0:T(8,128)S(1)}, u32[]{:S(2)}, u32[]{:S(2)}) collective-permute-start(f32[2,32,128]{2,1,0:T(8,128)S(1)} %pad_maximum_fusion.2), channel_id=1, source_target_pairs={{0,5},{1,4},{2,7},{3,6},{4,1},{5,0},{6,3},{7,2},{8,13},{9,12},{10,... | collective-permute-start | bytes 98312 | tf_op jit(solution)/shard_map/ppermute | solution.py:358
  24.6 0.5 %collective-permute-start.10 = (f32[2,32,128]{2,1,0:T(8,128)S(1)}, f32[2,32,128]{2,1,0:T(8,128)S(1)}, u32[]{:S(2)}, u32[]{:S(2)}) collective-permute-start(f32[2,32,128]{2,1,0:T(8,128)S(1)} %pad_maximum_fusion.1), channel_id=1, source_target_pairs={{0,4},{1,5},{2,6},{3,7},{4,0},{5,1},{6,2},{7,3},{8,12},{9,13},{10,... | collective-permute-start | bytes 98312 | tf_op jit(solution)/shard_map/ppermute | solution.py:358
  25.1 0.6 %collective-permute-start.8 = (f32[2,32,128]{2,1,0:T(8,128)S(1)}, f32[2,32,128]{2,1,0:T(8,128)S(1)}, u32[]{:S(2)}, u32[]{:S(2)}) collective-permute-start(f32[2,32,128]{2,1,0:T(8,128)S(1)} %pad_maximum_fusion), channel_id=1, source_target_pairs={{0,1},{1,0},{2,3},{3,2},{4,5},{5,4},{6,7},{7,6},{8,9},{9,8},{10,11... | collective-permute-start | bytes 98312 | tf_op jit(solution)/shard_map/ppermute | solution.py:358
  25.7 1.2 %collective-permute-done.11.refs_2_ = f32[2,32,128]{2,1,0:T(8,128)S(1)} collective-permute-done((f32[2,32,128]{2,1,0:T(8,128)S(1)}, f32[2,32,128]{2,1,0:T(8,128)S(1)}, u32[]{:S(2)}, u32[]{:S(2)}) %collective-permute-start.11) | collective-permute-done | bytes 32800 | tf_op jit(solution)/shard_map/ppermute | solution.py:358
  26.9 1.6 %collective-permute-done.10.refs_1_ = f32[2,32,128]{2,1,0:T(8,128)S(1)} collective-permute-done((f32[2,32,128]{2,1,0:T(8,128)S(1)}, f32[2,32,128]{2,1,0:T(8,128)S(1)}, u32[]{:S(2)}, u32[]{:S(2)}) %collective-permute-start.10) | collective-permute-done | bytes 32800 | tf_op jit(solution)/shard_map/ppermute | solution.py:358
  28.5 0.6 %collective-permute-done.8.refs_0_ = f32[2,32,128]{2,1,0:T(8,128)S(1)} collective-permute-done((f32[2,32,128]{2,1,0:T(8,128)S(1)}, f32[2,32,128]{2,1,0:T(8,128)S(1)}, u32[]{:S(2)}, u32[]{:S(2)}) %collective-permute-start.8) | collective-permute-done | bytes 32800 | tf_op jit(solution)/shard_map/ppermute | solution.py:358
  29.1 1.4 %doppler.1 = f32[2048,128]{1,0:T(8,128)} custom-call(f32[32,128]{1,0:T(8,128)S(1)} %get-tuple-element.25.keep_ref, f32[2,32,128]{2,1,0:T(8,128)S(1)} %collective-permute-done.7.recv_ref, f32[2,32,128]{2,1,0:T(8,128)S(1)} %collective-permute-done.8.refs_0_, f32[2,32,128]{2,1,0:T(8,128)S(1)} %collective-permute-done.10.refs_1_, ...), custom_call_target="tpu_custom_call" | custom-call | tf_op jit(solution)/shard_map/doppler/pallas_call | solution.py:472
  (33 shorter events, 1.4 us)
Async XLA Ops:
  0.0 14.6 %copy-start.1 = (bf16[1024,256]{1,0:T(8,128)(2,1)S(1)}, bf16[1024,256]{1,0:T(8,128)(2,1)}, u32[]{:S(2)}) copy-start(bf16[1024,256]{1,0:T(8,128)(2,1)} %constant.78.clone.refs_4_.table_low) | copy-start | bytes 1572868
  1.2 13.4 %copy-start = (bf16[1024,256]{1,0:T(8,128)(2,1)S(1)}, bf16[1024,256]{1,0:T(8,128)(2,1)}, u32[]{:S(2)}) copy-start(bf16[1024,256]{1,0:T(8,128)(2,1)} %constant.77.clone.refs_3_.table_high) | copy-start | bytes 1572868
  1.2 13.4 %collective-permute-start.2 = (f32[2,128,128]{2,1,0:T(8,128)S(1)}, f32[2,128,128]{2,1,0:T(8,128)S(1)}, u32[]{:S(2)}, u32[]{:S(2)}) collective-permute-start(f32[2,128,128]{2,1,0:T(8,128)S(1)} %get-tuple-element.34), channel_id=1, source_target_pairs={{0,2},{1,3},{2,0},{3,1},{4,6},{5,7},{6,4},{7,5},{8,10},{9,11},{10,... | collective-permute-start | bytes 393224 | tf_op jit(solution)/shard_map/ppermute | solution.py:358
  1.8 14.5 %collective-permute-start.5 = (f32[2,128,128]{2,1,0:T(8,128)S(1)}, f32[2,128,128]{2,1,0:T(8,128)S(1)}, u32[]{:S(2)}, u32[]{:S(2)}) collective-permute-start(f32[2,128,128]{2,1,0:T(8,128)S(1)} %get-tuple-element.34), channel_id=1, source_target_pairs={{0,10},{1,11},{2,8},{3,9},{4,14},{5,15},{6,12},{7,13},{8,18},{9,19... | collective-permute-start | bytes 393224 | tf_op jit(solution)/shard_map/ppermute | solution.py:358
  4.4 5.5 %collective-permute-start.3 = (f32[2,128,128]{2,1,0:T(8,128)S(1)}, f32[2,128,128]{2,1,0:T(8,128)S(1)}, u32[]{:S(2)}, u32[]{:S(2)}) collective-permute-start(f32[2,128,128]{2,1,0:T(8,128)S(1)} %get-tuple-element.33), channel_id=1, source_target_pairs={{0,4},{1,5},{2,6},{3,7},{4,0},{5,1},{6,2},{7,3},{8,12},{9,13},{10,... | collective-permute-start | bytes 393224 | tf_op jit(solution)/shard_map/ppermute | solution.py:358
  6.0 9.9 %collective-permute-start.4 = (f32[2,128,128]{2,1,0:T(8,128)S(1)}, f32[2,128,128]{2,1,0:T(8,128)S(1)}, u32[]{:S(2)}, u32[]{:S(2)}) collective-permute-start(f32[2,128,128]{2,1,0:T(8,128)S(1)} %get-tuple-element.35.refs_0_), channel_id=1, source_target_pairs={{0,8},{1,9},{2,10},{3,11},{4,12},{5,13},{6,14},{7,15},{8,16},{9,17... | collective-permute-start | bytes 393224 | tf_op jit(solution)/shard_map/ppermute | solution.py:358
  7.5 5.5 %collective-permute-start = (f32[2,128,128]{2,1,0:T(8,128)S(1)}, f32[2,128,128]{2,1,0:T(8,128)S(1)}, u32[]{:S(2)}, u32[]{:S(2)}) collective-permute-start(f32[2,128,128]{2,1,0:T(8,128)S(1)} %get-tuple-element.36), channel_id=1, source_target_pairs={{0,6},{1,7},{2,4},{3,5},{4,2},{5,3},{6,0},{7,1},{8,14},{9,15},{10,... | collective-permute-start | bytes 393224 | tf_op jit(solution)/shard_map/ppermute | solution.py:358
  9.9 7.7 %collective-permute-start.6 = (f32[2,128,128]{2,1,0:T(8,128)S(1)}, f32[2,128,128]{2,1,0:T(8,128)S(1)}, u32[]{:S(2)}, u32[]{:S(2)}) collective-permute-start(f32[2,128,128]{2,1,0:T(8,128)S(1)} %collective-permute-done.3.refs_2_), channel_id=1, source_target_pairs={{0,8},{1,9},{2,10},{3,11},{4,12},{5,13},{6,14},{7,15},{8,16},{9,17... | collective-permute-start | bytes 393224 | tf_op jit(solution)/shard_map/ppermute | solution.py:358
  13.0 7.0 %collective-permute-start.1 = (f32[2,128,128]{2,1,0:T(8,128)S(1)}, f32[2,128,128]{2,1,0:T(8,128)S(1)}, u32[]{:S(2)}, u32[]{:S(2)}) collective-permute-start(f32[2,128,128]{2,1,0:T(8,128)S(1)} %collective-permute-done.piece), channel_id=1, source_target_pairs={{0,8},{1,9},{2,10},{3,11},{4,12},{5,13},{6,14},{7,15},{8,16},{9,17... | collective-permute-start | bytes 393224 | tf_op jit(solution)/shard_map/ppermute | solution.py:358
  17.7 2.4 %copy-start.2 = (bf16[1024,256]{1,0:T(8,128)(2,1)S(1)}, bf16[1024,256]{1,0:T(8,128)(2,1)}, u32[]{:S(2)}) copy-start(bf16[1024,256]{1,0:T(8,128)(2,1)} %constant.79.clone.t_high) | copy-start | bytes 1572868
  17.7 2.4 %copy-start.3 = (bf16[1024,256]{1,0:T(8,128)(2,1)S(1)}, bf16[1024,256]{1,0:T(8,128)(2,1)}, u32[]{:S(2)}) copy-start(bf16[1024,256]{1,0:T(8,128)(2,1)} %constant.80.clone.t_low) | copy-start | bytes 1572868
  20.8 1.3 %collective-permute-start.9 = (f32[2,32,128]{2,1,0:T(8,128)S(1)}, f32[2,32,128]{2,1,0:T(8,128)S(1)}, u32[]{:S(2)}, u32[]{:S(2)}) collective-permute-start(f32[2,32,128]{2,1,0:T(8,128)S(1)} %get-tuple-element.29), channel_id=1, source_target_pairs={{0,2},{1,3},{2,0},{3,1},{4,6},{5,7},{6,4},{7,5},{8,10},{9,11},{10,... | collective-permute-start | bytes 98312 | tf_op jit(solution)/shard_map/ppermute | solution.py:358
  21.3 3.8 %collective-permute-start.7 = (f32[2,32,128]{2,1,0:T(8,128)S(1)}, f32[2,32,128]{2,1,0:T(8,128)S(1)}, u32[]{:S(2)}, u32[]{:S(2)}) collective-permute-start(f32[2,32,128]{2,1,0:T(8,128)S(1)} %get-tuple-element.26), channel_id=1, source_target_pairs={{0,2},{1,3},{2,0},{3,1},{4,6},{5,7},{6,4},{7,5},{8,10},{9,11},{10,... | collective-permute-start | bytes 98312 | tf_op jit(solution)/shard_map/ppermute | solution.py:358
  22.0 4.9 %collective-permute-start.11 = (f32[2,32,128]{2,1,0:T(8,128)S(1)}, f32[2,32,128]{2,1,0:T(8,128)S(1)}, u32[]{:S(2)}, u32[]{:S(2)}) collective-permute-start(f32[2,32,128]{2,1,0:T(8,128)S(1)} %pad_maximum_fusion.2), channel_id=1, source_target_pairs={{0,5},{1,4},{2,7},{3,6},{4,1},{5,0},{6,3},{7,2},{8,13},{9,12},{10,... | collective-permute-start | bytes 98312 | tf_op jit(solution)/shard_map/ppermute | solution.py:358
  24.6 3.9 %collective-permute-start.10 = (f32[2,32,128]{2,1,0:T(8,128)S(1)}, f32[2,32,128]{2,1,0:T(8,128)S(1)}, u32[]{:S(2)}, u32[]{:S(2)}) collective-permute-start(f32[2,32,128]{2,1,0:T(8,128)S(1)} %pad_maximum_fusion.1), channel_id=1, source_target_pairs={{0,4},{1,5},{2,6},{3,7},{4,0},{5,1},{6,2},{7,3},{8,12},{9,13},{10,... | collective-permute-start | bytes 98312 | tf_op jit(solution)/shard_map/ppermute | solution.py:358
  25.1 4.0 %collective-permute-start.8 = (f32[2,32,128]{2,1,0:T(8,128)S(1)}, f32[2,32,128]{2,1,0:T(8,128)S(1)}, u32[]{:S(2)}, u32[]{:S(2)}) collective-permute-start(f32[2,32,128]{2,1,0:T(8,128)S(1)} %pad_maximum_fusion), channel_id=1, source_target_pairs={{0,1},{1,0},{2,3},{3,2},{4,5},{5,4},{6,7},{7,6},{8,9},{9,8},{10,11... | collective-permute-start | bytes 98312 | tf_op jit(solution)/shard_map/ppermute | solution.py:358
